TPU v7x, 32 devices: a whole 2x2x4 slice. The times are simulated.
32 devices in a mesh: groups: 2 (over y), ctx: 4 (over z), exp: 2 (over x), head: 2 (over core).
Axes of the slice: x: 2, y: 2, z: 4, core: 2. Of those that a mesh axis runs over, the one named last changes fastest.
Arguments:
- latent: bfloat16 [256, 576], P(('groups', 'ctx')), parts along dimension 0, may hold values from -5 to 5
- query: bfloat16 [256, 3072], P(('groups', 'ctx'), ('exp', 'head')), parts along dimension 0, may hold values from -30 to 30
- w_uk: bfloat16 [512, 2048], P(None, ('exp', 'head')), may hold values from -0.25 to 0.25
- w_uv: bfloat16 [512, 2048], P(None, ('exp', 'head')), may hold values from -0.25 to 0.25
- w_o: bfloat16 [2048, 3584], P(('exp', 'head'), 'ctx'), may hold values from -0.5 to 0.5
- resid: bfloat16 [256, 3584], P(('groups', 'ctx', 'exp', 'head')), parts along dimension 0, may hold values from -6 to 6
- norm_gain: float32 [3584], replicated, may hold values from 0.1 to 1.9
- w_gate: bfloat16 [4, 3584, 2048], P(('exp', 'head'), None, 'ctx'), may hold values from -0.09375 to 0.09375
- w_up: bfloat16 [4, 3584, 2048], P(('exp', 'head'), None, 'ctx'), may hold values from -0.09375 to 0.09375
- w_down: bfloat16 [4, 2048, 3584], P(('exp', 'head'), None, 'ctx'), may hold values from -0.125 to 0.125
- expert_ids: int32 [256, 2], P(('groups', 'ctx', 'exp', 'head')), parts along dimension 0, may hold values from 0 to 3, all different within a row; in each aligned block of 8 rows (0 to 7, 8 to 15, ...) at most 8 rows name the same one
- route_weights: float32 [256, 2], P(('groups', 'ctx', 'exp', 'head')), parts along dimension 0, may hold values from 0.2 to 1
Outputs:
- layer_out: bfloat16 [256, 3584], P(('groups', 'ctx', 'exp', 'head')), parts along dimension 0
There are 2 independent parts, one for each index of `groups`. A program takes and returns all parts, laid end to end along the dimension named above; an argument that names none is the same for every part. Nothing has to cross between parts.
Inputs may be any that keep to these rules, and one draw needn't show every extreme that they name: `expert_ids`: each token names 2 different experts; within each aligned block of 8 tokens no expert is named more than 8 times, a bound that some block reaches.
All inputs are finite; a program needn't handle non-finite values.
Results may differ from a plain program's by a relative error of at most 0.014.
Values may be sent and summed in bfloat16 or wider, within the bound.
A program may use at most 64 MiB of HBM per device.

v0:
```python
import math
import jax
import jax.numpy as jnp
from jax import lax
from jax.sharding import PartitionSpec as P

D = 3584
NOPE = 128
ROPE = 64
LATENT = 512


def shards(
    latent,
    query,
    w_uk,
    w_uv,
    w_o,
    resid,
    norm_gain,
    w_gate,
    w_up,
    w_down,
    expert_ids,
    route_weights,
):
    qblock = query.shape[0]
    head_width = NOPE + ROPE
    heads_here = query.shape[1] // head_width
    nope_span = heads_here * NOPE
    score_scale = 1.0 / math.sqrt(head_width)
    query_all = query.reshape(qblock, heads_here, head_width)
    query_nope = query_all[:, :, :NOPE]
    query_rope = query_all[:, :, NOPE:]
    query_pos = lax.axis_index("ctx") * qblock + jnp.arange(qblock, dtype=jnp.int32)
    shard_rows = lax.all_gather(latent, "ctx", axis=0, tiled=True)
    piece_rows = shard_rows.shape[0]
    compressed = shard_rows[:, :LATENT]
    key_nope = (
        jnp.dot(compressed, w_uk, preferred_element_type=jnp.float32)
        .astype(jnp.bfloat16)
        .reshape(piece_rows, heads_here, NOPE)
    )
    values = (
        jnp.dot(compressed, w_uv, preferred_element_type=jnp.float32)
        .astype(jnp.bfloat16)
        .reshape(piece_rows, heads_here, NOPE)
    )
    run_max = jnp.full((qblock, heads_here), -1e30, jnp.float32)
    piece_rows = key_nope.shape[0]
    scores = jnp.einsum("qhd,khd->qhk", query_nope, key_nope, preferred_element_type=jnp.float32)
    scores = (
        scores
        + jnp.einsum(
            "qhd,kd->qhk", query_rope, shard_rows[:, LATENT:], preferred_element_type=jnp.float32
        )
    ) * score_scale
    key_pos = jnp.arange(piece_rows, dtype=jnp.int32)
    allowed = (key_pos[None, :] <= query_pos[:, None])[:, None, :]
    new_max = jnp.maximum(run_max, jnp.max(jnp.where(allowed, scores, -1e30), axis=2))
    exponent = jnp.where(allowed, jnp.exp(scores - new_max[:, :, None]), 0.0)
    run_sum = jnp.sum(exponent, axis=2)
    weighted_sum = jnp.einsum(
        "qhk,khd->qhd", exponent.astype(jnp.bfloat16), values, preferred_element_type=jnp.float32
    )
    attn_state = (new_max, run_sum, weighted_sum)
    run_max, run_sum, weighted_sum = attn_state
    attended = (weighted_sum / run_sum[:, :, None]).astype(jnp.bfloat16).reshape(qblock, nope_span)
    tok_dev = resid.shape[0]
    ctx_count = lax.axis_size("ctx")
    partial_value = jnp.dot(
        lax.all_gather(attended, "ctx", axis=0, tiled=True), w_o, preferred_element_type=jnp.float32
    )
    partial_value = partial_value.astype(jnp.bfloat16).reshape(ctx_count, qblock, w_o.shape[1])
    summed = lax.psum_scatter(
        partial_value, ("exp", "head"), scatter_dimension=1, tiled=True
    ).astype(jnp.float32)
    swapped = lax.all_to_all(
        summed.astype(jnp.bfloat16), "ctx", split_axis=0, concat_axis=2, tiled=True
    ).astype(summed.dtype)
    projected = swapped.reshape(tok_dev, D)
    residual_sum = resid.astype(jnp.float32) + projected
    inverse_rms = lax.rsqrt(jnp.mean(residual_sum * residual_sum, axis=1, keepdims=True) + 1e-06)
    normalized = (residual_sum * inverse_rms * norm_gain).astype(jnp.bfloat16)
    experts = lax.axis_size(("exp", "head"))
    top_count = expert_ids.shape[1]
    capacity = max(2, 2 * tok_dev * top_count // experts)
    flat_ids = expert_ids.reshape(-1)
    onehot = (flat_ids[:, None] == jnp.arange(experts, dtype=jnp.int32)[None, :]).astype(jnp.int32)
    slot_rank = jnp.sum((jnp.cumsum(onehot, axis=0) - onehot) * onehot, axis=1)
    target = (flat_ids * capacity + slot_rank).reshape(tok_dev, top_count)
    slot_ids = jnp.arange(experts * capacity, dtype=jnp.int32)
    route_hits = (target[:, :, None] == slot_ids[None, None, :]).astype(jnp.float32)
    picker = jnp.sum(route_hits, axis=1).astype(jnp.bfloat16)
    dispatched = jnp.einsum(
        "ts,td->sd", picker, normalized, preferred_element_type=jnp.float32
    ).astype(jnp.bfloat16)
    outgoing = dispatched.reshape(experts, capacity, D)
    arrived = lax.all_to_all(outgoing, ("exp", "head"), split_axis=0, concat_axis=0, tiled=True)
    rows_in = arrived.reshape(experts * capacity, D)
    gate_local = w_gate[0]
    up_local = w_up[0]
    down_local = w_down[0]
    shard_rows = lax.all_gather(rows_in, "ctx", axis=0, tiled=True)
    gate_part = jnp.dot(shard_rows, gate_local, preferred_element_type=jnp.float32)
    up_part = jnp.dot(shard_rows, up_local, preferred_element_type=jnp.float32)
    hidden_cols = (jax.nn.silu(gate_part) * up_part).astype(jnp.bfloat16)
    expert_cols = jnp.dot(
        lax.all_gather(hidden_cols, "ctx", axis=1, tiled=True),
        down_local,
        preferred_element_type=jnp.float32,
    ).astype(jnp.bfloat16)
    returned = lax.all_to_all(
        expert_cols.reshape(ctx_count, experts * capacity, down_local.shape[1]),
        "ctx",
        split_axis=0,
        concat_axis=2,
        tiled=True,
    )
    returned_rows = lax.all_to_all(
        returned.reshape(experts, capacity, D),
        ("exp", "head"),
        split_axis=0,
        concat_axis=0,
        tiled=True,
    )
    returned_rows = returned_rows.reshape(experts * capacity, D)
    weighted = jnp.sum(route_hits * route_weights[:, :, None], axis=1)
    moe_sum = jnp.dot(weighted, returned_rows.astype(jnp.float32), precision=lax.Precision.HIGHEST)
    return (residual_sum + moe_sum).astype(jnp.bfloat16)


def solution(mesh):
    placed = (
        P(("groups", "ctx"), None),
        P(("groups", "ctx"), ("exp", "head")),
        P(None, ("exp", "head")),
        P(None, ("exp", "head")),
        P(("exp", "head"), "ctx"),
        P(("groups", "ctx", "exp", "head"), None),
        P(),
        P(("exp", "head"), None, "ctx"),
        P(("exp", "head"), None, "ctx"),
        P(("exp", "head"), None, "ctx"),
        P(("groups", "ctx", "exp", "head"), None),
        P(("groups", "ctx", "exp", "head"), None),
    )
    return jax.shard_map(
        shards,
        mesh=mesh,
        in_specs=placed,
        out_specs=P(("groups", "ctx", "exp", "head"), None),
        check_vma=False,
    )
```

profile of v0, /device:TPU:0, one launch (start us, length us, event | category | flops | bytes accessed | tf_op | source)
XLA Modules:
  0.0 148.8 jit_solution(2626256943590443223)
XLA Ops:
  6.5 0.0 copy-start
  6.5 0.0 reduce-scatter.4.cloned.1.call-start
  6.6 1.0 reshape.85
  7.6 0.1 iota_compare_fusion
  7.7 15.4 %all_gather.12 = bf16[128,576]{1,0:T(8,128)(2,1)S(1)} all-gather(bf16[32,576]{1,0:T(8,128)(2,1)} %param.12), channel_id=1, replica_groups=mesh['groups'=2,'ctx'=4,'exp'=2,'head'=2] {'ctx'}, dimensions={0}, use_global_device_ids=true | all-gather | bytes 184320 | tf_op jit(solution)/shard_map/all_gather | solution.py:36
  23.1 1.3 fusion.19
  24.4 1.3 fusion.18
  25.7 0.2 convolution_bitcast_fusion.1
  25.8 0.3 select_reduce_fusion
  26.1 0.2 convolution_bitcast_fusion
  26.3 0.3 fusion.23
  26.7 13.5 %all_gather.13 = bf16[128,512]{1,0:T(8,128)(2,1)S(1)} all-gather(bf16[32,512]{1,0:T(8,128)(2,1)S(1)} %bitcast.80), channel_id=1, replica_groups=mesh['groups'=2,'ctx'=4,'exp'=2,'head'=2] {'ctx'}, dimensions={0}, use_global_device_ids=true | all-gather | bytes 163840 | tf_op jit(solution)/shard_map/all_gather | solution.py:72
  40.2 0.0 copy-done
  40.2 0.3 convolution_convert_fusion.1
  40.5 0.1 copy.49
  40.6 0.7 copy.57
  41.3 0.0 reduce-scatter.4.cloned.1.call-update
  41.4 0.0 copy-done.4
  41.4 0.1 copy.45
  41.5 0.1 eq.28
  41.5 0.1 fusion.44
  41.6 0.2 select_reduce_fusion.2
  41.8 0.1 reduce_sum.49
  41.9 0.1 copy.47
  42.0 20.8 %reduce-scatter.4.cloned.1.call-done = bf16[8,3584]{1,0:T(8,128)(2,1)} async-done(((bf16[32,3584]{1,0:T(8,128)(2,1)}), bf16[8,3584]{1,0:T(8,128)(2,1)}) %reduce-scatter.4.cloned.1.call-update) | async-done | bytes 57360
  62.8 0.8 reshape.97
  63.6 0.6 copy.50
  64.3 4.6 %all-to-all-start = ((bf16[4,8,896]{2,1,0:T(8,128)(2,1)}), bf16[4,8,896]{2,1,0:T(8,128)(2,1)S(1)}, u32[]{:S(2)}, u32[]{:S(2)}) async-start(bf16[4,8,896]{2,1,0:T(8,128)(2,1)} %copy.50), calls=%async_computation | async-start | bytes 114688 | tf_op jit(solution)/shard_map/all_to_all | solution.py:78
  68.9 0.0 copy-done.5
  68.9 0.1 convert_reduce_fusion
  68.9 5.6 %all-to-all-done = bf16[4,8,896]{2,1,0:T(8,128)(2,1)S(1)} async-done(((bf16[4,8,896]{2,1,0:T(8,128)(2,1)}), bf16[4,8,896]{2,1,0:T(8,128)(2,1)S(1)}, u32[]{:S(2)}, u32[]{:S(2)}) %all-to-all-start) | async-done | bytes 57376 | tf_op jit(solution)/shard_map/all_to_all | solution.py:78
  74.6 0.0 copy-done.2
  74.6 0.1 multiply_reduce_fusion
  74.8 0.0 copy-done.3
  74.8 0.3 fusion.1
  75.0 8.2 %all_to_all.34 = bf16[4,8,3584]{2,1,0:T(8,128)(2,1)S(1)} all-to-all(bf16[4,8,3584]{2,1,0:T(8,128)(2,1)S(1)} %fusion.1), channel_id=1, replica_groups=mesh['groups'=2,'ctx'=4,'exp'=2,'head'=2] {'exp','head'}, dimensions={0} | all-to-all | bytes 458752 | tf_op jit(solution)/shard_map/all_to_all | solution.py:99
  83.2 19.1 %all_gather.14 = bf16[128,3584]{1,0:T(8,128)(2,1)S(1)} all-gather(bf16[32,3584]{1,0:T(8,128)(2,1)S(1)} %bitcast.77), channel_id=1, replica_groups=mesh['groups'=2,'ctx'=4,'exp'=2,'head'=2] {'ctx'}, dimensions={0}, use_global_device_ids=true | all-gather | bytes 1146880 | tf_op jit(solution)/shard_map/all_gather | solution.py:104
  102.3 2.7 %fusion.7 = f32[128,512]{1,0:T(8,128)S(1)} fusion(bf16[128,3584]{1,0:T(8,128)(2,1)S(1)} %all_gather.14, bf16[1,3584,512]{2,1,0:T(8,128)(2,1)} %param.19), kind=kOutput, calls=%fused_computation.9 | convolution fusion | flops 469762048 | bytes 4849664 | tf_op jit(solution)/shard_map/dot_general | solution.py:105
  104.9 0.0 copy-done.6
  105.0 0.0 copy-start.1
  105.0 0.6 fusion.15
  105.6 15.8 %all_gather.15 = bf16[128,2048]{1,0:T(8,128)(2,1)S(1)} all-gather(bf16[128,512]{1,0:T(8,128)(2,1)S(1)} %fusion.15), channel_id=1, replica_groups=mesh['groups'=2,'ctx'=4,'exp'=2,'head'=2] {'ctx'}, dimensions={1}, use_global_device_ids=true | all-gather | bytes 655360 | tf_op jit(solution)/shard_map/all_gather | solution.py:109
  121.4 0.7 fusion.9
  122.1 10.7 %all_to_all.35 = bf16[4,32,896]{2,1,0:T(8,128)(2,1)S(1)} all-to-all(bf16[4,32,896]{2,1,0:T(8,128)(2,1)S(1)} %bitcast.78), channel_id=1, replica_groups=mesh['groups'=2,'ctx'=4,'exp'=2,'head'=2] {'ctx'}, dimensions={0} | all-to-all | bytes 458752 | tf_op jit(solution)/shard_map/all_to_all | solution.py:113
  132.9 0.1 copy.48
  133.0 0.1 reshape.91
  133.1 8.0 %all_to_all.36 = bf16[4,8,3584]{2,1,0:T(8,128)(2,1)S(1)} all-to-all(bf16[4,8,3584]{2,1,0:T(8,128)(2,1)S(1)} %reshape.91), channel_id=1, replica_groups=mesh['groups'=2,'ctx'=4,'exp'=2,'head'=2] {'exp','head'}, dimensions={0} | all-to-all | bytes 458752 | tf_op jit(solution)/shard_map/all_to_all | solution.py:120
  141.1 0.8 fusion.2
  (15 shorter events, 0.1 us)
Async XLA Ops:
  6.5 33.7 %copy-start = (bf16[512,896]{1,0:T(8,128)(2,1)S(1)}, bf16[512,896]{1,0:T(8,128)(2,1)}, u32[]{:S(2)}) copy-start(bf16[512,896]{1,0:T(8,128)(2,1)} %param.16) | copy-start | bytes 2752516
  6.5 34.8 %copy-start.4 = (s32[8,2]{0,1:T(2,128)S(1)}, s32[8,2]{0,1:T(2,128)}, u32[]{:S(2)}) copy-start(s32[8,2]{0,1:T(2,128)} %param.22) | copy-start | bytes 196
  6.5 62.3 %copy-start.5 = (f32[8,2]{0,1:T(2,128)S(1)}, f32[8,2]{0,1:T(2,128)}, u32[]{:S(2)}) copy-start(f32[8,2]{0,1:T(2,128)} %param.23) | copy-start | bytes 196
  6.5 68.1 %copy-start.2 = (bf16[8,3584]{1,0:T(8,128)(2,1)S(1)}, bf16[8,3584]{1,0:T(8,128)(2,1)}, u32[]{:S(2)}) copy-start(bf16[8,3584]{1,0:T(8,128)(2,1)} %param.17) | copy-start | bytes 172036
  6.5 68.2 %copy-start.3 = (f32[3584]{0:T(1024)S(1)}, f32[3584]{0:T(1024)}, u32[]{:S(2)}) copy-start(f32[3584]{0:T(1024)} %param.18) | copy-start | bytes 43012
  6.5 56.2 %reduce-scatter.4.cloned.1.call-start = ((), (), s32[]{:S(2)}) async-start(), calls=%async_computation.5 | async-start | bytes 286720
  64.3 10.3 %all-to-all-start = ((bf16[4,8,896]{2,1,0:T(8,128)(2,1)}), bf16[4,8,896]{2,1,0:T(8,128)(2,1)S(1)}, u32[]{:S(2)}, u32[]{:S(2)}) async-start(bf16[4,8,896]{2,1,0:T(8,128)(2,1)} %copy.50), calls=%async_computation | async-start | bytes 114688 | tf_op jit(solution)/shard_map/all_to_all | solution.py:78
  74.6 30.4 %copy-start.6 = (bf16[1,3584,512]{2,1,0:T(8,128)(2,1)S(1)}, bf16[1,3584,512]{2,1,0:T(8,128)(2,1)}, u32[]{:S(2)}) copy-start(bf16[1,3584,512]{2,1,0:T(8,128)(2,1)} %param.20) | copy-start | bytes 11010052
  105.0 16.4 %copy-start.1 = (bf16[1,2048,896]{2,1,0:T(8,128)(2,1)S(1)}, bf16[1,2048,896]{2,1,0:T(8,128)(2,1)}, u32[]{:S(2)}) copy-start(bf16[1,2048,896]{2,1,0:T(8,128)(2,1)} %param.21) | copy-start | bytes 11010052
Sparse Core Ops, SparseCore 0:
  41.5 21.2 reduce-scatter.3
where the time goes:
time: 149 us
  blocking collectives  90.6 us (61%)
  waiting for transfers between devices  26.4 us (18%)
  between operations  13.6 us (9%)
  matrix products  8.65 us (6%)
  starting transfers between devices  4.63 us (3%)
  local copies, waits for them, and re-layouts  3.88 us (3%)
    unnamed x2, waiting for transfers between devices  20.8 us
    all_gather x1, blocking collectives, shards(): shard_rows = lax.all_gather(rows_in, 'ctx', axis=0, tiled=True)  19.1 us
    all_gather x1, blocking collectives, shards(): lax.all_gather(hidden_cols, 'ctx', axis=1, tiled=True)  15.8 us
    all_gather x1, blocking collectives, shards(): shard_rows = lax.all_gather(latent, 'ctx', axis=0, tiled=True)  15.4 us
    all_gather x1, blocking collectives, shards(): lax.all_gather(attended, 'ctx', axis=0, tiled=True)  13.5 us
    all_to_all x1, blocking collectives, shards(): lax.all_to_all(expert_cols.reshape(ctx_count, experts * capacity, down_lo...  10.7 us
    all_to_all x1, blocking collectives, shards(): lax.all_to_all(outgoing, ('exp', 'head'), split_axis=0, concat_axis=0, ti...  8.16 us
    all_to_all x1, blocking collectives, shards(): lax.all_to_all(returned.reshape(experts, capacity, D), ('exp', 'head'), s...  8.03 us
  transfers between devices with their start and end apart: 2, of which 2 were waited for; matrix products, arithmetic and copies ran while one was open for 0% of the time, Pallas kernels for 0%

commit v1 on v0

--- a/solution.py
+++ b/solution.py
@@ -8,6 +8,28 @@
 NOPE = 128
 ROPE = 64
 LATENT = 512
+
+
+def split_up(array, dim, size):
+    before, after = (array.shape[:dim], array.shape[dim + 1 :])
+    return jnp.moveaxis(array.reshape(*before, size, -1, *after), dim, 0)
+
+
+def laid_out(parts, dim):
+    dims = list(parts.shape[1:])
+    dims[dim] *= parts.shape[0]
+    return jnp.moveaxis(parts, 0, dim).reshape(dims)
+
+
+def exchange_in_pairs(shard, axis, split_dim, concat_dim):
+    devices, index = (lax.axis_size(axis), lax.axis_index(axis))
+    parts = split_up(shard, split_dim, devices)
+    done = [parts[index]]
+    for step in range(1, devices):
+        sent = parts[index ^ step]
+        done.append(lax.ppermute(sent, axis, [(i, i ^ step) for i in range(devices)]))
+    parts = jnp.stack(done)[index ^ jnp.arange(devices)]
+    return laid_out(parts, concat_dim)
 
 
 def shards(
@@ -75,9 +97,7 @@
     summed = lax.psum_scatter(
         partial_value, ("exp", "head"), scatter_dimension=1, tiled=True
     ).astype(jnp.float32)
-    swapped = lax.all_to_all(
-        summed.astype(jnp.bfloat16), "ctx", split_axis=0, concat_axis=2, tiled=True
-    ).astype(summed.dtype)
+    swapped = exchange_in_pairs(summed.astype(jnp.bfloat16), "ctx", 0, 2).astype(summed.dtype)
     projected = swapped.reshape(tok_dev, D)
     residual_sum = resid.astype(jnp.float32) + projected
     inverse_rms = lax.rsqrt(jnp.mean(residual_sum * residual_sum, axis=1, keepdims=True) + 1e-06)

time: 149 us -> 147 us (0.987)
  waiting for transfers between devices: 26.4 us -> 24.2 us
    all_to_all x1 -> x0, waiting for transfers between devices: 5.64 us -> none  [shards(): lax.all_to_all(summed.astype(jnp.bfloat16), 'ctx', split_axis=0, concat_a...]
    all_to_all x1 -> x0, starting transfers between devices: 4.59 us -> none  [shards(): lax.all_to_all(summed.astype(jnp.bfloat16), 'ctx', split_axis=0, concat_a...]
    ppermute x0 -> x3, starting transfers between devices: none -> 4.45 us  [exchange_in_pairs(): lax.ppermute(sent, axis, [(i, i ^ step) for i in range(devices)])]
    ppermute x0 -> x3, waiting for transfers between devices: none -> 3.54 us  [exchange_in_pairs(): lax.ppermute(sent, axis, [(i, i ^ step) for i in range(devices)])]
  transfers between devices with their start and end apart: 2 -> 4, of which waited for: 2 -> 4; matrix products, arithmetic and copies ran while one was open for 0% -> 0% of each run, Pallas kernels for 0% -> 0%
where the time goes in v1:
time: 147 us
  blocking collectives  90.8 us (62%)
  waiting for transfers between devices  24.2 us (16%)
  between operations  13.7 us (9%)
  matrix products  8.65 us (6%)
  starting transfers between devices  4.49 us (3%)
  local copies, waits for them, and re-layouts  3.96 us (3%)
    unnamed x2, waiting for transfers between devices  20.7 us
    all_gather x1, blocking collectives, shards(): shard_rows = lax.all_gather(rows_in, 'ctx', axis=0, tiled=True)  19.7 us
    all_gather x1, blocking collectives, shards(): lax.all_gather(hidden_cols, 'ctx', axis=1, tiled=True)  16 us
    all_gather x1, blocking collectives, shards(): shard_rows = lax.all_gather(latent, 'ctx', axis=0, tiled=True)  15.4 us
    all_gather x1, blocking collectives, shards(): lax.all_gather(attended, 'ctx', axis=0, tiled=True)  13.5 us
    all_to_all x1, blocking collectives, shards(): lax.all_to_all(expert_cols.reshape(ctx_count, experts * capacity, down_lo...  9.98 us
    all_to_all x1, blocking collectives, shards(): lax.all_to_all(outgoing, ('exp', 'head'), split_axis=0, concat_axis=0, ti...  8.16 us
    all_to_all x1, blocking collectives, shards(): lax.all_to_all(returned.reshape(experts, capacity, D), ('exp', 'head'), s...  8.03 us
  transfers between devices with their start and end apart: 4, of which 4 were waited for; matrix products, arithmetic and copies ran while one was open for 0% of the time, Pallas kernels for 0%

profile of v1, /device:TPU:0, one launch (start us, length us, event | category | flops | bytes accessed | tf_op | source)
XLA Modules:
  0.0 146.8 jit_solution(5247143959769553894)
XLA Ops:
  6.5 0.0 reduce-scatter.4.cloned.1.call-start
  6.6 1.0 reshape.108
  7.7 0.1 iota_compare_fusion
  7.7 15.4 %all_gather.12 = bf16[128,576]{1,0:T(8,128)(2,1)S(1)} all-gather(bf16[32,576]{1,0:T(8,128)(2,1)} %param.12), channel_id=1, replica_groups=mesh['groups'=2,'ctx'=4,'exp'=2,'head'=2] {'ctx'}, dimensions={0}, use_global_device_ids=true | all-gather | bytes 184320 | tf_op jit(solution)/shard_map/all_gather | solution.py:58
  23.1 1.3 fusion.19
  24.4 1.3 fusion.18
  25.7 0.2 convolution_bitcast_fusion.1
  25.8 0.3 select_reduce_fusion
  26.1 0.2 convolution_bitcast_fusion
  26.3 0.3 fusion.23
  26.7 13.5 %all_gather.13 = bf16[128,512]{1,0:T(8,128)(2,1)S(1)} all-gather(bf16[32,512]{1,0:T(8,128)(2,1)S(1)} %bitcast.90), channel_id=1, replica_groups=mesh['groups'=2,'ctx'=4,'exp'=2,'head'=2] {'ctx'}, dimensions={0}, use_global_device_ids=true | all-gather | bytes 163840 | tf_op jit(solution)/shard_map/all_gather | solution.py:94
  40.2 0.3 convolution_convert_fusion.1
  40.5 0.1 copy.49
  40.6 0.7 copy.61
  41.3 0.0 reduce-scatter.4.cloned.1.call-update
  41.4 0.1 copy.45
  41.5 0.1 eq.28
  41.5 0.1 fusion.44
  41.6 0.2 select_reduce_fusion.2
  41.8 0.1 reduce_sum.49
  41.9 0.1 copy.47
  42.0 0.1 convert_reduce_fusion
  42.1 20.7 %reduce-scatter.4.cloned.1.call-done = bf16[8,3584]{1,0:T(8,128)(2,1)} async-done(((bf16[32,3584]{1,0:T(8,128)(2,1)}), bf16[8,3584]{1,0:T(8,128)(2,1)}) %reduce-scatter.4.cloned.1.call-update) | async-done | bytes 57360
  62.8 0.8 reshape.130
  63.6 0.1 constant_dynamic-slice_fusion.3
  63.8 3.4 %collective-permute-start.2 = (bf16[1,8,896]{2,1,0:T(8,128)(2,1)S(1)}, bf16[1,8,896]{2,1,0:T(8,128)(2,1)S(1)}, u32[]{:S(2)}, u32[]{:S(2)}) collective-permute-start(bf16[1,8,896]{2,1,0:T(8,128)(2,1)S(1)} %copy.57), channel_id=1, source_target_pairs={{0,12},{4,8},{8,4},{12,0},{1,13},{5,9},{9,5},{13,1},{2,14},{6,10},... | collective-permute-start | bytes 43016 | tf_op jit(solution)/shard_map/ppermute | solution.py:30
  67.2 0.0 collective-permute-start
  67.2 1.1 collective-permute-start.1
  68.3 1.1 collective-permute-done.2
  69.4 1.5 %collective-permute-done = bf16[1,8,896]{2,1,0:T(8,128)(2,1)S(1)} collective-permute-done((bf16[1,8,896]{2,1,0:T(8,128)(2,1)S(1)}, bf16[1,8,896]{2,1,0:T(8,128)(2,1)S(1)}, u32[]{:S(2)}, u32[]{:S(2)}) %collective-permute-start) | collective-permute-done | bytes 14368 | tf_op jit(solution)/shard_map/ppermute | solution.py:30
  70.9 0.9 collective-permute-done.1
  71.8 0.6 gather_fusion
  72.4 0.0 copy-start.6
  72.4 0.1 multiply_reduce_fusion
  72.6 0.0 copy-done.3
  72.6 0.3 fusion.1
  72.9 8.2 %all_to_all.25 = bf16[4,8,3584]{2,1,0:T(8,128)(2,1)S(1)} all-to-all(bf16[4,8,3584]{2,1,0:T(8,128)(2,1)S(1)} %fusion.1), channel_id=1, replica_groups=mesh['groups'=2,'ctx'=4,'exp'=2,'head'=2] {'exp','head'}, dimensions={0} | all-to-all | bytes 458752 | tf_op jit(solution)/shard_map/all_to_all | solution.py:119
  81.0 19.7 %all_gather.14 = bf16[128,3584]{1,0:T(8,128)(2,1)S(1)} all-gather(bf16[32,3584]{1,0:T(8,128)(2,1)S(1)} %bitcast.87), channel_id=1, replica_groups=mesh['groups'=2,'ctx'=4,'exp'=2,'head'=2] {'ctx'}, dimensions={0}, use_global_device_ids=true | all-gather | bytes 1146880 | tf_op jit(solution)/shard_map/all_gather | solution.py:124
  100.7 2.7 %fusion.7 = f32[128,512]{1,0:T(8,128)S(1)} fusion(bf16[128,3584]{1,0:T(8,128)(2,1)S(1)} %all_gather.14, bf16[1,3584,512]{2,1,0:T(8,128)(2,1)} %param.19), kind=kOutput, calls=%fused_computation.10 | convolution fusion | flops 469762048 | bytes 4849664 | tf_op jit(solution)/shard_map/dot_general | solution.py:125
  103.4 0.0 copy-start.1
  103.4 0.6 fusion.15
  104.1 16.0 %all_gather.15 = bf16[128,2048]{1,0:T(8,128)(2,1)S(1)} all-gather(bf16[128,512]{1,0:T(8,128)(2,1)S(1)} %fusion.15), channel_id=1, replica_groups=mesh['groups'=2,'ctx'=4,'exp'=2,'head'=2] {'ctx'}, dimensions={1}, use_global_device_ids=true | all-gather | bytes 655360 | tf_op jit(solution)/shard_map/all_gather | solution.py:129
  120.1 0.7 fusion.9
  120.8 10.0 %all_to_all.26 = bf16[4,32,896]{2,1,0:T(8,128)(2,1)S(1)} all-to-all(bf16[4,32,896]{2,1,0:T(8,128)(2,1)S(1)} %bitcast.88), channel_id=1, replica_groups=mesh['groups'=2,'ctx'=4,'exp'=2,'head'=2] {'ctx'}, dimensions={0} | all-to-all | bytes 458752 | tf_op jit(solution)/shard_map/all_to_all | solution.py:133
  130.8 0.1 copy.48
  131.0 0.1 reshape.114
  131.0 8.0 %all_to_all.27 = bf16[4,8,3584]{2,1,0:T(8,128)(2,1)S(1)} all-to-all(bf16[4,8,3584]{2,1,0:T(8,128)(2,1)S(1)} %reshape.114), channel_id=1, replica_groups=mesh['groups'=2,'ctx'=4,'exp'=2,'head'=2] {'exp','head'}, dimensions={0} | all-to-all | bytes 458752 | tf_op jit(solution)/shard_map/all_to_all | solution.py:140
  139.1 0.8 fusion.2
  (27 shorter events, 0.2 us)
Async XLA Ops:
  6.5 33.7 %copy-start = (bf16[512,896]{1,0:T(8,128)(2,1)S(1)}, bf16[512,896]{1,0:T(8,128)(2,1)}, u32[]{:S(2)}) copy-start(bf16[512,896]{1,0:T(8,128)(2,1)} %param.16) | copy-start | bytes 2752516
  6.5 34.8 %copy-start.4 = (s32[8,2]{0,1:T(2,128)S(1)}, s32[8,2]{0,1:T(2,128)}, u32[]{:S(2)}) copy-start(s32[8,2]{0,1:T(2,128)} %param.22) | copy-start | bytes 196
  6.5 35.5 %copy-start.5 = (f32[8,2]{0,1:T(2,128)S(1)}, f32[8,2]{0,1:T(2,128)}, u32[]{:S(2)}) copy-start(f32[8,2]{0,1:T(2,128)} %param.23) | copy-start | bytes 196
  6.5 65.9 %copy-start.2 = (bf16[8,3584]{1,0:T(8,128)(2,1)S(1)}, bf16[8,3584]{1,0:T(8,128)(2,1)}, u32[]{:S(2)}) copy-start(bf16[8,3584]{1,0:T(8,128)(2,1)} %param.17) | copy-start | bytes 172036
  6.5 66.0 %copy-start.3 = (f32[3584]{0:T(1024)S(1)}, f32[3584]{0:T(1024)}, u32[]{:S(2)}) copy-start(f32[3584]{0:T(1024)} %param.18) | copy-start | bytes 43012
  6.5 56.2 %reduce-scatter.4.cloned.1.call-start = ((), (), s32[]{:S(2)}) async-start(), calls=%async_computation.4 | async-start | bytes 286720
  63.8 5.6 %collective-permute-start.2 = (bf16[1,8,896]{2,1,0:T(8,128)(2,1)S(1)}, bf16[1,8,896]{2,1,0:T(8,128)(2,1)S(1)}, u32[]{:S(2)}, u32[]{:S(2)}) collective-permute-start(bf16[1,8,896]{2,1,0:T(8,128)(2,1)S(1)} %copy.57), channel_id=1, source_target_pairs={{0,12},{4,8},{8,4},{12,0},{1,13},{5,9},{9,5},{13,1},{2,14},{6,10},... | collective-permute-start | bytes 43016 | tf_op jit(solution)/shard_map/ppermute | solution.py:30
  67.2 3.7 %collective-permute-start = (bf16[1,8,896]{2,1,0:T(8,128)(2,1)S(1)}, bf16[1,8,896]{2,1,0:T(8,128)(2,1)S(1)}, u32[]{:S(2)}, u32[]{:S(2)}) collective-permute-start(bf16[1,8,896]{2,1,0:T(8,128)(2,1)S(1)} %copy.55), channel_id=1, source_target_pairs={{0,4},{4,0},{8,12},{12,8},{1,5},{5,1},{9,13},{13,9},{2,6},{6,2},{1... | collective-permute-start | bytes 43016 | tf_op jit(solution)/shard_map/ppermute | solution.py:30
  67.2 4.6 %collective-permute-start.1 = (bf16[1,8,896]{2,1,0:T(8,128)(2,1)S(1)}, bf16[1,8,896]{2,1,0:T(8,128)(2,1)S(1)}, u32[]{:S(2)}, u32[]{:S(2)}) collective-permute-start(bf16[1,8,896]{2,1,0:T(8,128)(2,1)S(1)} %copy.56), channel_id=1, source_target_pairs={{0,8},{4,12},{8,0},{12,4},{1,9},{5,13},{9,1},{13,5},{2,10},{6,14},... | collective-permute-start | bytes 43016 | tf_op jit(solution)/shard_map/ppermute | solution.py:30
  72.4 31.0 %copy-start.6 = (bf16[1,3584,512]{2,1,0:T(8,128)(2,1)S(1)}, bf16[1,3584,512]{2,1,0:T(8,128)(2,1)}, u32[]{:S(2)}) copy-start(bf16[1,3584,512]{2,1,0:T(8,128)(2,1)} %param.20) | copy-start | bytes 11010052
  103.4 16.7 %copy-start.1 = (bf16[1,2048,896]{2,1,0:T(8,128)(2,1)S(1)}, bf16[1,2048,896]{2,1,0:T(8,128)(2,1)}, u32[]{:S(2)}) copy-start(bf16[1,2048,896]{2,1,0:T(8,128)(2,1)} %param.21) | copy-start | bytes 11010052
Sparse Core Ops, SparseCore 0:
  41.5 21.2 reduce-scatter.3
